TPU v7x, 128 devices: a whole 4x4x4 slice. The times are simulated.
128 devices in a mesh: seq: 8 (over y, x_hi), hid: 16 (over z, x_lo, core).
Axes of the slice: x: 4 (x_hi: 2, x_lo: 2; x = x_hi * 2 + x_lo), y: 4, z: 4, core: 2. Of those that a mesh axis runs over, the one named last changes fastest.
Arguments:
- tokens: bfloat16 [5120, 5120], P('seq', 'hid'), may hold values from -18 to 18
- clip_id: int32 [5120], P('seq'), may hold values from 0 to 7, never falling along the last dimension, each value on 1 to 3200 neighbouring positions
- clip_step: int32 [8], replicated, may hold values from 0 to 31
- mod_table: float32 [32, 6, 5120], replicated, may hold values from -3 to 3
- w_query: bfloat16 [5120, 4096], P(None, 'hid'), may hold values from -3 to 3
- w_key: bfloat16 [5120, 4096], P(None, 'hid'), may hold values from -3 to 3
- w_value: bfloat16 [5120, 4096], P(None, 'hid'), may hold values from -0.078125 to 0.078125
- q_gain: float32 [4096], P('hid'), may hold values from 0.4 to 6
- k_gain: float32 [4096], P('hid'), may hold values from 0.4 to 6
- w_out: bfloat16 [4096, 5120], P('hid'), may hold values from -0.125 to 0.125
- w_up: bfloat16 [5120, 8192], P(None, 'hid'), may hold values from -0.078125 to 0.078125
- w_down: bfloat16 [8192, 5120], P('hid'), may hold values from -0.09375 to 0.09375
Outputs:
- block_out: bfloat16 [5120, 5120], P('seq', 'hid')
Inputs may be any that keep to these rules, and one draw needn't show every extreme that they name: `clip_id`: clip numbers never fall along the tokens; every clip 0 to 7 holds 1 to 3200 tokens, and one holds exactly 3200.
All inputs are finite; a program needn't handle non-finite values.
Results may differ from a plain program's by a relative error of at most 0.018.
Values may be sent and summed in bfloat16 or wider, within the bound.
A program may use at most 128 MiB of HBM per device.

v0:
```python
import jax
import jax.numpy as jnp
from jax import lax
from jax.sharding import PartitionSpec as P

HEAD_DIM = 128
epsilon = 1e-06
highest = lax.Precision.HIGHEST
masked_low = -1e30


def table_rows(step_hot, mod_table, component, col_start, col_count):
    table = lax.dynamic_slice_in_dim(mod_table[:, component, :], col_start, col_count, 1)
    return jnp.dot(step_hot, table, precision=highest, preferred_element_type=jnp.float32)


def modulated(values, row_mean, spread_sq, scale_rows, shift_rows):
    scaled = (values - row_mean) * lax.rsqrt(spread_sq + epsilon)
    return (scaled * (1.0 + scale_rows) + shift_rows).astype(jnp.bfloat16)


def shared_moments(values, full_width):
    summed, squares = lax.psum((jnp.sum(values, axis=1), jnp.sum(values * values, axis=1)), "hid")
    row_mean = (summed / full_width)[:, None]
    return (row_mean, (squares / full_width)[:, None] - row_mean * row_mean)


def stored(values):
    return lax.optimization_barrier(values.astype(jnp.bfloat16)).astype(jnp.float32)


def shards(
    tokens,
    clip_id,
    clip_step,
    mod_table,
    w_query,
    w_key,
    w_value,
    q_gain,
    k_gain,
    w_out,
    w_up,
    w_down,
):
    tok_rows, feat_part = tokens.shape
    full_width = mod_table.shape[2]
    col_start = lax.axis_index("hid") * feat_part
    head_cols = w_query.shape[1]
    heads_here = head_cols // HEAD_DIM
    all_cols = head_cols * lax.axis_size("hid")
    clip_hot = (
        clip_id[:, None] == jnp.arange(clip_step.shape[0], dtype=jnp.int32)[None, :]
    ).astype(jnp.float32)
    token_step = jnp.dot(
        clip_hot,
        clip_step.astype(jnp.float32),
        precision=highest,
        preferred_element_type=jnp.float32,
    )
    step_hot = (
        token_step[:, None] == jnp.arange(mod_table.shape[0], dtype=jnp.float32)[None, :]
    ).astype(jnp.float32)
    own_rows = tokens.astype(jnp.float32)
    gate_ffn = table_rows(step_hot, mod_table, 5, col_start, feat_part)
    row_mean, spread_sq = shared_moments(own_rows, full_width)
    normed = modulated(
        own_rows,
        row_mean,
        spread_sq,
        table_rows(step_hot, mod_table, 1, col_start, feat_part),
        table_rows(step_hot, mod_table, 0, col_start, feat_part),
    )
    pieces = lax.all_gather(normed, "hid", axis=1, tiled=True)

    def accumulate(weight):
        return jnp.dot(pieces, weight, preferred_element_type=jnp.float32)

    queries = accumulate(w_query)
    key_proj = accumulate(w_key)
    value_proj = accumulate(w_value)
    q_sq, k_sq = lax.psum(
        (jnp.sum(queries * queries, axis=1), jnp.sum(key_proj * key_proj, axis=1)), "hid"
    )
    q_normed = (queries * lax.rsqrt(q_sq / all_cols + epsilon)[:, None] * q_gain).astype(
        jnp.bfloat16
    )
    k_normed = (key_proj * lax.rsqrt(k_sq / all_cols + epsilon)[:, None] * k_gain).astype(
        jnp.bfloat16
    )
    value_rows = value_proj.astype(jnp.bfloat16)
    clip_marks = clip_id.astype(jnp.bfloat16)
    q_heads = q_normed.reshape(tok_rows, heads_here, HEAD_DIM)
    score_scale = HEAD_DIM ** (-0.5)

    def tile_update(running, tile):
        key_tile, value_tile, mark_tile = tile
        old_best, old_sum, old_acc = running
        scores = (
            jnp.einsum("qhd,khd->hqk", q_heads, key_tile, preferred_element_type=jnp.float32)
            * score_scale
        )
        same_clip = (clip_marks[:, None] == mark_tile[None, :])[None]
        masked = jnp.where(same_clip, scores, masked_low)
        row_best = jnp.maximum(old_best, jnp.max(masked, axis=2))
        weights = jnp.where(same_clip, jnp.exp(masked - row_best[:, :, None]), 0.0)
        rescale = jnp.exp(old_best - row_best)
        new_sum = old_sum * rescale + jnp.sum(weights, axis=2)
        mixed = jnp.einsum(
            "hqk,khd->hqd",
            weights.astype(jnp.bfloat16),
            value_tile,
            preferred_element_type=jnp.float32,
        )
        return (row_best, new_sum, old_acc * rescale[:, :, None] + mixed)

    start_state = (
        jnp.full((heads_here, tok_rows), masked_low, jnp.float32),
        jnp.zeros((heads_here, tok_rows), jnp.float32),
        jnp.zeros((heads_here, tok_rows, HEAD_DIM), jnp.float32),
    )
    key_piece = lax.all_gather(k_normed, "seq", axis=0, tiled=True)
    value_piece = lax.all_gather(value_rows, "seq", axis=0, tiled=True)
    mark_piece = lax.all_gather(clip_marks, "seq", axis=0, tiled=True)
    tile_count = key_piece.shape[0] // tok_rows
    tiles = (
        key_piece.reshape(tile_count, tok_rows, heads_here, HEAD_DIM),
        value_piece.reshape(tile_count, tok_rows, heads_here, HEAD_DIM),
        mark_piece.reshape(tile_count, tok_rows),
    )

    def tile_step(inner, tile):
        return (tile_update(inner, tile), None)

    finished, unused = lax.scan(tile_step, start_state, tiles)
    best_all, sum_all, acc_all = finished
    attended = (
        (acc_all / sum_all[:, :, None])
        .astype(jnp.bfloat16)
        .transpose(1, 0, 2)
        .reshape(tok_rows, head_cols)
    )
    out_terms = jnp.dot(attended, w_out, preferred_element_type=jnp.float32)
    attn_own = lax.psum_scatter(
        out_terms.astype(jnp.bfloat16), "hid", scatter_dimension=1, tiled=True
    ).astype(jnp.float32)
    gate_attn = table_rows(step_hot, mod_table, 2, col_start, feat_part)
    residual_own = stored(own_rows + gate_attn * attn_own)
    row_mean, spread_sq = shared_moments(residual_own, full_width)
    normed_ffn = modulated(
        residual_own,
        row_mean,
        spread_sq,
        table_rows(step_hot, mod_table, 4, col_start, feat_part),
        table_rows(step_hot, mod_table, 3, col_start, feat_part),
    )
    up_proj = jnp.dot(
        lax.all_gather(normed_ffn, "hid", axis=1, tiled=True),
        w_up,
        preferred_element_type=jnp.float32,
    )
    hidden = jax.nn.gelu(up_proj, approximate=True).astype(jnp.bfloat16)
    ffn_own = lax.psum_scatter(
        jnp.dot(hidden, w_down, preferred_element_type=jnp.float32).astype(jnp.bfloat16),
        "hid",
        scatter_dimension=1,
        tiled=True,
    ).astype(jnp.float32)
    return (residual_own + gate_ffn * ffn_own).astype(jnp.bfloat16)


def solution(mesh):
    placed = (
        P("seq", "hid"),
        P("seq"),
        P(),
        P(),
        P(None, "hid"),
        P(None, "hid"),
        P(None, "hid"),
        P("hid"),
        P("hid"),
        P("hid", None),
        P(None, "hid"),
        P("hid", None),
    )
    return jax.shard_map(
        shards, mesh=mesh, in_specs=placed, out_specs=P("seq", "hid"), check_vma=False
    )
```

profile of v0, /device:TPU:0, one launch (start us, length us, event | category | flops | bytes accessed | tf_op | source)
XLA Modules:
  0.0 604.5 jit_solution(17240052192492611231)
XLA Ops:
  7.9 4.1 fusion.72
  11.9 32.1 %all-reduce.2 = (f32[640]{0:T(1024)S(1)}, f32[640]{0:T(1024)S(1)}) all-reduce(f32[640]{0:T(1024)S(1)} %get-tuple-element.124, f32[640]{0:T(1024)S(1)} %get-tuple-element.123), channel_id=1, replica_groups=mesh['seq'=8,'hid'=16] {'hid'}, use_global_device_ids=true, to_apply=%region_3.0 | all-reduce | flops 1280 | bytes 10240 | tf_op jit(solution)/shard_map/psum | solution.py:23
  48.5 42.2 %all-gather.6.cloned.1.call-done = bf16[640,5120]{0,1:T(8,128)(2,1)} async-done(((bf16[640,320]{0,1:T(8,128)(2,1)}), bf16[640,5120]{0,1:T(8,128)(2,1)}) %all-gather.6.cloned.1.call-update) | async-done | bytes 6553616 | tf_op jit(solution)/shard_map/all_gather | solution.py:74
  90.7 6.0 multiply_reduce_fusion.1
  97.0 3.1 multiply_reduce_fusion
  100.1 30.5 %all-reduce.1 = (f32[640]{0:T(1024)S(1)}, f32[640]{0:T(1024)S(1)}) all-reduce(f32[640]{0:T(1024)S(1)} %get-tuple-element.163, f32[640]{0:T(1024)S(1)} %get-tuple-element.165), channel_id=1, replica_groups=mesh['seq'=8,'hid'=16] {'hid'}, use_global_device_ids=true, to_apply=%region_5.0 | all-reduce | flops 1280 | bytes 10240 | tf_op jit(solution)/shard_map/psum | solution.py:82
  131.6 6.3 %convolution_convert_fusion.2 = bf16[640,256]{1,0:T(8,128)(2,1)} fusion(bf16[640,5120]{0,1:T(8,128)(2,1)} %all-gather.6.cloned.1.call-done, bf16[5120,256]{1,0:T(8,128)(2,1)} %param.20), kind=kOutput, calls=%fused_computation.56 | convolution fusion | flops 1677885440 | bytes 9502720 | tf_op jit(solution)/shard_map/dot_general | solution.py:77
  138.0 34.2 %all-gather = bf16[8,1,640]{2,1,0:T(2,128)(2,1)S(1)} all-gather(bf16[1,1,640]{2,1,0:T(2,128)(2,1)S(1)} %reshape.75), channel_id=1, replica_groups=mesh['seq'=8,'hid'=16] {'seq'}, dimensions={0}, use_global_device_ids=true | all-gather | bytes 11520 | tf_op jit(solution)/shard_map/all_gather | solution.py:124
  173.6 14.6 %all-gather.8.cloned.1.call-done = bf16[5120,256]{0,1:T(8,128)(2,1)} async-done(((bf16[640,256]{0,1:T(8,128)(2,1)}), bf16[5120,256]{0,1:T(8,128)(2,1)}) %all-gather.8.cloned.1.call-update) | async-done | bytes 2621456 | tf_op jit(solution)/shard_map/all_gather | solution.py:122
  188.2 3.8 copy.35
  192.0 4.8 copy.28
  196.7 49.9 %all-gather.10.cloned.1.call-done = bf16[5120,256]{1,0:T(8,128)(2,1)} async-done(((bf16[640,256]{1,0:T(8,128)(2,1)}), bf16[5120,256]{1,0:T(8,128)(2,1)}) %all-gather.10.cloned.1.call-update) | async-done | bytes 2621456 | tf_op jit(solution)/shard_map/all_gather | solution.py:123
  246.7 4.9 reshape.73
  251.6 84.6 %while.15 = (s32[]{:T(128)}, f32[2,640]{1,0:T(2,128)S(1)}, f32[2,640]{1,0:T(2,128)S(1)}, f32[2,640,128]{2,1,0:T(8,128)}, bf16[640]{0:T(1024)(128)(2,1)S(1)}, /*i...) while((s32[]{:T(128)}, f32[2,640]{1,0:T(2,128)S(1)}, ...), condition=%wide.region_11.12_spmd.clone, body=%wide.region_8.11_spmd.clone.sunk | while | flops 430987520 | bytes 32855764 | solution.py:135
  252.0 3.5 fusion.95
  255.5 2.9 fusion.97
  262.5 3.5 fusion.95
  266.1 2.9 fusion.97
  273.1 3.5 fusion.95
  276.7 2.9 fusion.97
  283.7 3.5 fusion.95
  294.3 3.5 fusion.95
  304.8 3.5 fusion.95
  315.4 3.5 fusion.95
  326.0 3.5 fusion.95
  337.6 5.0 convolution_convert_fusion
  342.7 77.5 %reduce-scatter.3.cloned.1.call-done = bf16[640,320]{0,1:T(8,128)(2,1)} async-done(((bf16[640,5120]{0,1:T(8,128)(2,1)}), bf16[640,320]{0,1:T(8,128)(2,1)}) %reduce-scatter.3.cloned.1.call-update) | async-done | bytes 409616 | tf_op jit(solution)/shard_map/reduce_scatter | solution.py:144
  422.2 29.1 %all-reduce = (f32[640]{0:T(1024)S(1)}, f32[640]{0:T(1024)S(1)}) all-reduce(f32[640]{0:T(1024)S(1)} %get-tuple-element.122, f32[640]{0:T(1024)S(1)} %get-tuple-element.121), channel_id=1, replica_groups=mesh['seq'=8,'hid'=16] {'hid'}, use_global_device_ids=true, to_apply=%region_16.17 | all-reduce | flops 1280 | bytes 10240 | tf_op jit(solution)/shard_map/psum | solution.py:23
  455.6 41.8 %all-gather.12.cloned.1.call-done = bf16[640,5120]{0,1:T(8,128)(2,1)} async-done(((bf16[640,320]{0,1:T(8,128)(2,1)}), bf16[640,5120]{0,1:T(8,128)(2,1)}) %all-gather.12.cloned.1.call-update) | async-done | bytes 6553616 | tf_op jit(solution)/shard_map/all_gather | solution.py:158
  497.4 7.6 %fusion.73 = f32[640,512]{1,0:T(8,128)S(1)} fusion(bf16[640,5120]{0,1:T(8,128)(2,1)} %all-gather.12.cloned.1.call-done, bf16[5120,512]{1,0:T(8,128)(2,1)} %param.24), kind=kOutput, calls=%fused_computation.112 | convolution fusion | flops 3355443200 | bytes 13107200 | tf_op jit(solution)/shard_map/dot_general | solution.py:157
  505.0 9.5 %convolution_convert_fusion.1 = bf16[640,5120]{0,1:T(8,128)(2,1)} fusion(bf16[512,5120]{1,0:T(8,128)(2,1)} %param.25, f32[640,512]{1,0:T(8,128)S(1)} %fusion.73), kind=kOutput, calls=%fused_computation.26 | convolution fusion | flops 3361669120 | bytes 13107200 | tf_op jit(solution)/shard_map/dot_general | solution.py:164
  514.5 80.6 %reduce-scatter.5.cloned.1.call-done = bf16[640,320]{0,1:T(8,128)(2,1)} async-done(((bf16[640,5120]{0,1:T(8,128)(2,1)}), bf16[640,320]{0,1:T(8,128)(2,1)}) %reduce-scatter.5.cloned.1.call-update) | async-done | bytes 409616 | tf_op jit(solution)/shard_map/reduce_scatter | solution.py:163
  (163 shorter events, 65.5 us)
Async XLA Ops:
  6.5 331.1 %copy-start = (bf16[256,5120]{1,0:T(8,128)(2,1)S(1)}, bf16[256,5120]{1,0:T(8,128)(2,1)}, u32[]{:S(2)}) copy-start(bf16[256,5120]{1,0:T(8,128)(2,1)} %param.23) | copy-start | bytes 7864324
  6.5 84.2 %all-gather.6.cloned.1.call-start = ((), (), s32[]{:S(2)}) async-start(), calls=%async_computation.2 | async-start | bytes 6963200 | tf_op jit(solution)/shard_map/all_gather | solution.py:74
  7.8 36.2 %copy-start.7 = (s32[640]{0:T(1024)S(1)}, s32[640]{0:T(1024)}, u32[]{:S(2)}) copy-start(s32[640]{0:T(1024)} %param.15) | copy-start | bytes 7684
  7.8 36.2 %copy-start.11 = (s32[8]{0:T(128)S(1)}, s32[8]{0:T(128)}, u32[]{:S(2)}) copy-start(s32[8]{0:T(128)} %param.16) | copy-start | bytes 100
  7.8 36.6 %copy-start.3 = (bf16[640,320]{0,1:T(8,128)(2,1)S(1)}, bf16[640,320]{0,1:T(8,128)(2,1)}, u32[]{:S(2)}) copy-start(bf16[640,320]{0,1:T(8,128)(2,1)} %param.14) | copy-start | bytes 1228804
  48.4 139.7 %all-gather.8.cloned.1.call-start = ((), (), s32[]{:S(2)}) async-start(), calls=%async_computation.3 | async-start | bytes 2949120 | tf_op jit(solution)/shard_map/all_gather | solution.py:122
  90.7 6.0 copy-start.2
  90.7 6.2 %copy-start.10 = (bf16[5120,256]{1,0:T(8,128)(2,1)S(1)}, bf16[5120,256]{1,0:T(8,128)(2,1)}, u32[]{:S(2)}) copy-start(bf16[5120,256]{1,0:T(8,128)(2,1)} %param.18) | copy-start | bytes 7864324
  97.0 33.7 %copy-start.8 = (f32[256]{0:T(256)S(1)}, f32[256]{0:T(256)}, u32[]{:S(2)}) copy-start(f32[256]{0:T(256)} %param.22) | copy-start | bytes 3076
  131.5 40.7 %copy-start.9 = (f32[256]{0:T(256)S(1)}, f32[256]{0:T(256)}, u32[]{:S(2)}) copy-start(f32[256]{0:T(256)} %param.21) | copy-start | bytes 3076
  131.5 115.1 %all-gather.10.cloned.1.call-start = ((), (), s32[]{:S(2)}) async-start(), calls=%async_computation.4 | async-start | bytes 2949120 | tf_op jit(solution)/shard_map/all_gather | solution.py:123
  137.9 282.4 %reduce-scatter.3.cloned.1.call-start = ((), (), s32[]{:S(2)}) async-start(), calls=%async_computation.5 | async-start | bytes 6963200 | tf_op jit(solution)/shard_map/reduce_scatter | solution.py:144
  255.5 4.2 copy-start.1
  255.5 4.2 copy-start.5
  266.1 4.2 copy-start.1
  266.1 4.2 copy-start.5
  276.6 4.2 copy-start.1
  276.7 4.2 copy-start.5
  282.5 0.8 copy-start.6
  287.2 4.2 copy-start.1
  287.2 4.2 copy-start.5
  297.8 4.2 copy-start.1
  297.8 4.2 copy-start.5
  308.4 4.2 copy-start.1
  308.4 4.2 copy-start.5
  319.0 4.2 copy-start.1
  319.0 4.2 copy-start.5
  329.5 4.2 copy-start.1
  329.6 4.2 copy-start.5
  342.7 77.6 %copy-start.4 = (bf16[640,320]{0,1:T(8,128)(2,1)S(1)}, bf16[640,320]{0,1:T(8,128)(2,1)}, u32[]{:S(2)}) copy-start(bf16[640,320]{0,1:T(8,128)(2,1)} %param.14) | copy-start | bytes 1228804
  342.7 154.7 %all-gather.12.cloned.1.call-start = ((), (), s32[]{:S(2)}) async-start(), calls=%async_computation.6 | async-start | bytes 6963200 | tf_op jit(solution)/shard_map/all_gather | solution.py:158
  455.3 139.8 %reduce-scatter.5.cloned.1.call-start = ((), (), s32[]{:S(2)}) async-start(), calls=%async_computation.7 | async-start | bytes 6963200 | tf_op jit(solution)/shard_map/reduce_scatter | solution.py:163
  (7 other events, 5.9 us)
Sparse Core Ops, SparseCore 0:
  48.6 42.1 all-gather.5
  131.6 56.4 all-gather.7
  190.5 56.1 all-gather.9
  342.8 77.3 reduce-scatter.2
  455.4 41.9 all-gather.11
  514.6 80.4 reduce-scatter.4
where the time goes:
time: 606 us; the launch traced here: 605 us
  waiting for transfers between devices  307 us (51%)
  blocking collectives  126 us (21%)
  matrix products  91.5 us (15%)
  local copies, waits for them, and re-layouts  36 us (6%)
  other arithmetic  29.8 us (5%)
  between operations  13.7 us (2%)
    reduce_scatter x1, waiting for transfers between devices, shards(): lax.psum_scatter(jnp.dot(hidden, w_down, preferred_element_type=jnp.float...  80.6 us
    reduce_scatter x1, waiting for transfers between devices, shards(): lax.psum_scatter(out_terms.astype(jnp.bfloat16), 'hid', scatter_dimension...  77.5 us
    psum x2, blocking collectives, shared_moments(): lax.psum((jnp.sum(values, axis=1), jnp.sum(values * values, axis=1)), 'hid')  61.2 us
    all_gather x1, waiting for transfers between devices, shards(): value_piece = lax.all_gather(value_rows, 'seq', axis=0, tiled=True)  49.9 us
    all_gather x1, waiting for transfers between devices, shards(): pieces = lax.all_gather(normed, 'hid', axis=1, tiled=True)  42.2 us
    all_gather x1, waiting for transfers between devices, shards(): lax.all_gather(normed_ffn, 'hid', axis=1, tiled=True)  41.8 us
    all_gather x1, blocking collectives, shards(): mark_piece = lax.all_gather(clip_marks, 'seq', axis=0, tiled=True)  34.2 us
    psum x1, blocking collectives, shards(): lax.psum((jnp.sum(queries * queries, axis=1), jnp.sum(key_proj * key_proj...  30.5 us
  transfers between devices with their start and end apart: 6, of which 6 were waited for; matrix products, arithmetic and copies ran while one was open for 3% of the time, Pallas kernels for 0%

commit v1 on v0

--- a/solution.py
+++ b/solution.py
@@ -119,7 +119,10 @@
         jnp.zeros((heads_here, tok_rows), jnp.float32),
         jnp.zeros((heads_here, tok_rows, HEAD_DIM), jnp.float32),
     )
-    key_piece = lax.all_gather(k_normed, "seq", axis=0, tiled=True)
+    count = lax.axis_size("seq")
+    parts = jnp.stack([k_normed for _ in range(count)])
+    parts = lax.all_to_all(parts, "seq", split_axis=0, concat_axis=0)
+    key_piece = jnp.concatenate(parts, axis=0)
     value_piece = lax.all_gather(value_rows, "seq", axis=0, tiled=True)
     mark_piece = lax.all_gather(clip_marks, "seq", axis=0, tiled=True)
     tile_count = key_piece.shape[0] // tok_rows

time: 606 us -> 565 us (0.932)
  waiting for transfers between devices: 307 us -> 240 us
  blocking collectives: 126 us -> 150 us
  local copies, waits for them, and re-layouts: 36 us -> 29.1 us
  starting transfers between devices: 0.43 us -> 7.29 us
    all_gather x1, waiting for transfers between devices: 49.9 us -> 0.02 us  [shards(): value_piece = lax.all_gather(value_rows, 'seq', axis=0, tiled=True)]
    all_gather x1, blocking collectives: 34.2 us -> 57.5 us  [shards(): mark_piece = lax.all_gather(clip_marks, 'seq', axis=0, tiled=True)]
    all_gather x1 -> x0, waiting for transfers between devices: 14.6 us -> none  [shards(): key_piece = lax.all_gather(k_normed, 'seq', axis=0, tiled=True)]
    unnamed x23 -> x19, local copies, waits for them, and re-layouts: 9.06 us -> 0.27 us
    all_to_all x0 -> x1, starting transfers between devices: none -> 6.91 us  [shards(): parts = lax.all_to_all(parts, 'seq', split_axis=0, concat_axis=0)]
  transfers between devices with their start and end apart: 6 -> 6, of which waited for: 6 -> 4; matrix products, arithmetic and copies ran while one was open for 3% -> 4% of each run, Pallas kernels for 0% -> 0%
where the time goes in v1:
time: 565 us; the launch traced here: 564 us
  waiting for transfers between devices  240 us (42%)
  blocking collectives  150 us (27%)
  matrix products  94.9 us (17%)
  local copies, waits for them, and re-layouts  29.1 us (5%)
  other arithmetic  29.1 us (5%)
  between operations  13.4 us (2%)
  starting transfers between devices  7.29 us (1%)
    reduce_scatter x1, waiting for transfers between devices, shards(): lax.psum_scatter(jnp.dot(hidden, w_down, preferred_element_type=jnp.float...  80.6 us
    reduce_scatter x1, waiting for transfers between devices, shards(): lax.psum_scatter(out_terms.astype(jnp.bfloat16), 'hid', scatter_dimension...  75.7 us
    psum x2, blocking collectives, shared_moments(): lax.psum((jnp.sum(values, axis=1), jnp.sum(values * values, axis=1)), 'hid')  61.2 us
    all_gather x1, blocking collectives, shards(): mark_piece = lax.all_gather(clip_marks, 'seq', axis=0, tiled=True)  57.5 us
    all_gather x1, waiting for transfers between devices, shards(): pieces = lax.all_gather(normed, 'hid', axis=1, tiled=True)  42.2 us
    all_gather x1, waiting for transfers between devices, shards(): lax.all_gather(normed_ffn, 'hid', axis=1, tiled=True)  41.8 us
    psum x1, blocking collectives, shards(): lax.psum((jnp.sum(queries * queries, axis=1), jnp.sum(key_proj * key_proj...  30.9 us
    dot_general x8, matrix products, tile_update(): jnp.einsum('qhd,khd->hqk', q_heads, key_tile, preferred_element_type=jnp....  28.9 us
  transfers between devices with their start and end apart: 6, of which 4 were waited for; matrix products, arithmetic and copies ran while one was open for 4% of the time, Pallas kernels for 0%

profile of v1, /device:TPU:0, one launch (start us, length us, event | category | flops | bytes accessed | tf_op | source)
XLA Modules:
  0.0 564.2 jit_solution(15628216427623157672)
XLA Ops:
  7.9 4.2 fusion.72
  12.1 32.1 %all-reduce.2 = (f32[640]{0:T(1024)S(1)}, f32[640]{0:T(1024)S(1)}) all-reduce(f32[640]{0:T(1024)S(1)} %get-tuple-element.124, f32[640]{0:T(1024)S(1)} %get-tuple-element.123), channel_id=1, replica_groups=mesh['seq'=8,'hid'=16] {'hid'}, use_global_device_ids=true, to_apply=%region_3.0 | all-reduce | flops 1280 | bytes 10240 | tf_op jit(solution)/shard_map/psum | solution.py:23
  48.7 42.2 %all-gather.5.cloned.1.call-done = bf16[640,5120]{0,1:T(8,128)(2,1)} async-done(((bf16[640,320]{0,1:T(8,128)(2,1)}), bf16[640,5120]{0,1:T(8,128)(2,1)}) %all-gather.5.cloned.1.call-update) | async-done | bytes 6553616 | tf_op jit(solution)/shard_map/all_gather | solution.py:74
  90.9 6.2 %convolution_convert_fusion.2 = bf16[640,256]{1,0:T(8,128)(2,1)} fusion(bf16[640,5120]{0,1:T(8,128)(2,1)} %all-gather.5.cloned.1.call-done, bf16[5120,256]{1,0:T(8,128)(2,1)} %param.20), kind=kOutput, calls=%fused_computation.56 | convolution fusion | flops 1677885440 | bytes 9502720 | tf_op jit(solution)/shard_map/dot_general | solution.py:77
  97.2 6.0 %multiply_reduce_fusion.1 = (f32[640]{0:T(1024)S(1)}, f32[640,256]{0,1:T(8,128)S(1)}) fusion(bf16[640,5120]{0,1:T(8,128)(2,1)} %all-gather.5.cloned.1.call-done, bf16[5120,256]{1,0:T(8,128)(2,1)} %param.19), kind=kOutput, calls=%fused_computation.70 | convolution fusion | flops 1678048640 | bytes 9832960 | tf_op jit(solution)/shard_map/dot_general | solution.py:77
  103.2 5.9 %multiply_reduce_fusion = (f32[640]{0:T(1024)S(1)}, f32[640,256]{0,1:T(8,128)}) fusion(bf16[640,5120]{0,1:T(8,128)(2,1)} %all-gather.5.cloned.1.call-done, bf16[5120,256]{1,0:T(8,128)(2,1)S(1)} %copy-done.9), kind=kOutput, calls=%fused_computation.68 | convolution fusion | flops 1678048640 | bytes 9832960 | tf_op jit(solution)/shard_map/dot_general | solution.py:77
  109.2 30.9 %all-reduce.1 = (f32[640]{0:T(1024)S(1)}, f32[640]{0:T(1024)S(1)}) all-reduce(f32[640]{0:T(1024)S(1)} %get-tuple-element.163, f32[640]{0:T(1024)S(1)} %get-tuple-element.165), channel_id=1, replica_groups=mesh['seq'=8,'hid'=16] {'hid'}, use_global_device_ids=true, to_apply=%region_5.0 | all-reduce | flops 1280 | bytes 10240 | tf_op jit(solution)/shard_map/psum | solution.py:82
  141.9 6.9 %all-to-all-start = ((bf16[8,640,256]{1,2,0:T(8,128)(2,1)}), bf16[8,640,256]{1,2,0:T(8,128)(2,1)}, u32[]{:S(2)}, u32[]{:S(2)}) async-start(bf16[8,640,256]{1,2,0:T(8,128)(2,1)} %stack.2), calls=%async_computation | async-start | bytes 5242880 | tf_op jit(solution)/shard_map/all_to_all | solution.py:124
  148.9 57.5 %all-gather = bf16[8,1,640]{2,1,0:T(2,128)(2,1)S(1)} all-gather(bf16[1,1,640]{2,1,0:T(2,128)(2,1)S(1)} %reshape.73), channel_id=1, replica_groups=mesh['seq'=8,'hid'=16] {'seq'}, dimensions={0}, use_global_device_ids=true | all-gather | bytes 11520 | tf_op jit(solution)/shard_map/all_gather | solution.py:127
  207.9 4.9 reshape.71
  212.9 85.2 %while.15 = (s32[]{:T(128)}, f32[2,640]{1,0:T(2,128)S(1)}, f32[2,640]{1,0:T(2,128)S(1)}, f32[2,640,128]{2,1,0:T(8,128)}, bf16[640]{0:T(1024)(128)(2,1)S(1)}, /*i...) while((s32[]{:T(128)}, f32[2,640]{1,0:T(2,128)S(1)}, ...), condition=%wide.region_11.12_spmd.clone, body=%wide.region_8.11_spmd.clone.sunk | while | flops 430987520 | bytes 32855764 | solution.py:138
  213.2 3.6 fusion.95
  216.8 2.9 fusion.97
  223.9 3.6 fusion.95
  227.5 2.9 fusion.97
  234.5 3.6 fusion.95
  245.2 3.6 fusion.95
  248.8 2.9 fusion.97
  255.8 3.6 fusion.95
  259.4 2.9 fusion.97
  266.5 3.6 fusion.95
  270.1 2.9 fusion.97
  277.1 3.6 fusion.95
  287.8 3.6 fusion.95
  291.4 2.9 fusion.97
  299.5 5.0 convolution_convert_fusion
  304.5 75.7 %reduce-scatter.3.cloned.1.call-done = bf16[640,320]{0,1:T(8,128)(2,1)} async-done(((bf16[640,5120]{0,1:T(8,128)(2,1)}), bf16[640,320]{0,1:T(8,128)(2,1)}) %reduce-scatter.3.cloned.1.call-update) | async-done | bytes 409616 | tf_op jit(solution)/shard_map/reduce_scatter | solution.py:147
  382.1 29.1 %all-reduce = (f32[640]{0:T(1024)S(1)}, f32[640]{0:T(1024)S(1)}) all-reduce(f32[640]{0:T(1024)S(1)} %get-tuple-element.122, f32[640]{0:T(1024)S(1)} %get-tuple-element.121), channel_id=1, replica_groups=mesh['seq'=8,'hid'=16] {'hid'}, use_global_device_ids=true, to_apply=%region_16.17 | all-reduce | flops 1280 | bytes 10240 | tf_op jit(solution)/shard_map/psum | solution.py:23
  415.5 41.8 %all-gather.9.cloned.1.call-done = bf16[640,5120]{0,1:T(8,128)(2,1)} async-done(((bf16[640,320]{0,1:T(8,128)(2,1)}), bf16[640,5120]{0,1:T(8,128)(2,1)}) %all-gather.9.cloned.1.call-update) | async-done | bytes 6553616 | tf_op jit(solution)/shard_map/all_gather | solution.py:161
  457.3 7.6 %fusion.73 = f32[640,512]{1,0:T(8,128)S(1)} fusion(bf16[640,5120]{0,1:T(8,128)(2,1)} %all-gather.9.cloned.1.call-done, bf16[5120,512]{1,0:T(8,128)(2,1)} %param.24), kind=kOutput, calls=%fused_computation.112 | convolution fusion | flops 3355443200 | bytes 13107200 | tf_op jit(solution)/shard_map/dot_general | solution.py:160
  464.9 9.6 %convolution_convert_fusion.1 = bf16[640,5120]{0,1:T(8,128)(2,1)} fusion(bf16[512,5120]{1,0:T(8,128)(2,1)} %param.25, f32[640,512]{1,0:T(8,128)S(1)} %fusion.73), kind=kOutput, calls=%fused_computation.26 | convolution fusion | flops 3361669120 | bytes 13107200 | tf_op jit(solution)/shard_map/dot_general | solution.py:167
  474.5 80.6 %reduce-scatter.5.cloned.1.call-done = bf16[640,320]{0,1:T(8,128)(2,1)} async-done(((bf16[640,5120]{0,1:T(8,128)(2,1)}), bf16[640,320]{0,1:T(8,128)(2,1)}) %reduce-scatter.5.cloned.1.call-update) | async-done | bytes 409616 | tf_op jit(solution)/shard_map/reduce_scatter | solution.py:166
  (158 shorter events, 57.4 us)
Async XLA Ops:
  6.5 292.9 %copy-start = (bf16[256,5120]{1,0:T(8,128)(2,1)S(1)}, bf16[256,5120]{1,0:T(8,128)(2,1)}, u32[]{:S(2)}) copy-start(bf16[256,5120]{1,0:T(8,128)(2,1)} %param.23) | copy-start | bytes 7864324
  6.5 84.4 %all-gather.5.cloned.1.call-start = ((), (), s32[]{:S(2)}) async-start(), calls=%async_computation.3 | async-start | bytes 6963200 | tf_op jit(solution)/shard_map/all_gather | solution.py:74
  7.8 36.4 %copy-start.6 = (s32[640]{0:T(1024)S(1)}, s32[640]{0:T(1024)}, u32[]{:S(2)}) copy-start(s32[640]{0:T(1024)} %param.15) | copy-start | bytes 7684
  7.8 36.4 %copy-start.10 = (s32[8]{0:T(128)S(1)}, s32[8]{0:T(128)}, u32[]{:S(2)}) copy-start(s32[8]{0:T(128)} %param.16) | copy-start | bytes 100
  7.8 36.8 %copy-start.2 = (bf16[640,320]{0,1:T(8,128)(2,1)S(1)}, bf16[640,320]{0,1:T(8,128)(2,1)}, u32[]{:S(2)}) copy-start(bf16[640,320]{0,1:T(8,128)(2,1)} %param.14) | copy-start | bytes 1228804
  48.6 159.3 %all-gather.7.cloned.1.call-start = ((), (), s32[]{:S(2)}) async-start(), calls=%async_computation.4 | async-start | bytes 2949120 | tf_op jit(solution)/shard_map/all_gather | solution.py:126
  97.2 6.0 %copy-start.9 = (bf16[5120,256]{1,0:T(8,128)(2,1)S(1)}, bf16[5120,256]{1,0:T(8,128)(2,1)}, u32[]{:S(2)}) copy-start(bf16[5120,256]{1,0:T(8,128)(2,1)} %param.18) | copy-start | bytes 7864324
  103.2 36.9 %copy-start.7 = (f32[256]{0:T(256)S(1)}, f32[256]{0:T(256)}, u32[]{:S(2)}) copy-start(f32[256]{0:T(256)} %param.22) | copy-start | bytes 3076
  141.9 64.6 %copy-start.8 = (f32[256]{0:T(256)S(1)}, f32[256]{0:T(256)}, u32[]{:S(2)}) copy-start(f32[256]{0:T(256)} %param.21) | copy-start | bytes 3076
  141.9 70.9 %all-to-all-start = ((bf16[8,640,256]{1,2,0:T(8,128)(2,1)}), bf16[8,640,256]{1,2,0:T(8,128)(2,1)}, u32[]{:S(2)}, u32[]{:S(2)}) async-start(bf16[8,640,256]{1,2,0:T(8,128)(2,1)} %stack.2), calls=%async_computation | async-start | bytes 5242880 | tf_op jit(solution)/shard_map/all_to_all | solution.py:124
  148.8 231.4 %reduce-scatter.3.cloned.1.call-start = ((), (), s32[]{:S(2)}) async-start(), calls=%async_computation.5 | async-start | bytes 6963200 | tf_op jit(solution)/shard_map/reduce_scatter | solution.py:147
  216.8 4.2 copy-start.1
  216.8 4.2 copy-start.4
  222.7 0.8 copy-start.5
  227.5 4.2 copy-start.1
  227.5 4.2 copy-start.4
  233.3 0.8 copy-start.5
  238.1 4.2 copy-start.1
  238.1 4.2 copy-start.4
  248.8 4.2 copy-start.1
  248.8 4.2 copy-start.4
  259.4 4.2 copy-start.1
  259.4 4.2 copy-start.4
  270.1 4.2 copy-start.1
  270.1 4.2 copy-start.4
  280.7 4.2 copy-start.1
  280.7 4.2 copy-start.4
  291.4 4.2 copy-start.1
  291.4 4.2 copy-start.4
  304.5 75.7 %copy-start.3 = (bf16[640,320]{0,1:T(8,128)(2,1)S(1)}, bf16[640,320]{0,1:T(8,128)(2,1)}, u32[]{:S(2)}) copy-start(bf16[640,320]{0,1:T(8,128)(2,1)} %param.14) | copy-start | bytes 1228804
  304.5 152.8 %all-gather.9.cloned.1.call-start = ((), (), s32[]{:S(2)}) async-start(), calls=%async_computation.6 | async-start | bytes 6963200 | tf_op jit(solution)/shard_map/all_gather | solution.py:161
  415.3 139.9 %reduce-scatter.5.cloned.1.call-start = ((), (), s32[]{:S(2)}) async-start(), calls=%async_computation.7 | async-start | bytes 6963200 | tf_op jit(solution)/shard_map/reduce_scatter | solution.py:166
  (6 other events, 5.1 us)
Sparse Core Ops, SparseCore 0:
  48.7 42.1 all-gather.4
  97.3 72.9 all-gather.6
  304.6 75.5 reduce-scatter.2
  415.4 41.9 all-gather.8
  474.6 80.4 reduce-scatter.4
